TPU v7x, 32 devices: a whole 2x2x4 slice. The times are simulated.
32 devices in a mesh: grp: 4 (over z), seq: 8 (over y, x, core).
Axes of the slice: x: 2, y: 2, z: 4, core: 2. Of those that a mesh axis runs over, the one named last changes fastest.
Arguments:
- tokens: bfloat16 [4096, 2048], P(('grp', 'seq')), may hold values from -6 to 6
- norm_gains: float32 [2, 2048], replicated, may hold values from 0.5 to 1.5
- norm_biases: float32 [2, 2048], replicated, may hold values from -1 to 1
- mix_weight: bfloat16 [2048, 3, 2048], P(None, None, 'seq'), may hold values from -0.125 to 0.125
- mix_bias: bfloat16 [3, 2048], P(None, 'seq'), may hold values from -1.796875 to 1.796875
- out_weight: bfloat16 [2048, 2048], P('seq'), may hold values from -0.5 to 0.5
- gate_up_weight: bfloat16 [2048, 2, 5632], P(None, None, 'seq'), may hold values from -0.125 to 0.125
- down_weight: bfloat16 [5632, 2048], P('seq'), may hold values from -0.078125 to 0.078125
- row_lengths: int32 [8], replicated, may hold values from 128 to 1024, as said below
- row_group: int32 [8], replicated, may hold values from 0 to 3, as said below
- cotangent: bfloat16 [4096, 2048], P(('grp', 'seq')), may hold values from -6 to 6
Outputs:
- layer_out: bfloat16 [4096, 2048], P(('grp', 'seq'))
- tokens_grad: bfloat16 [4096, 2048], P(('grp', 'seq'))
- gains_grad: float32 [2, 2048], replicated
- biases_grad: float32 [2, 2048], replicated
- mix_grad: float32 [2048, 3, 2048], P(None, None, 'seq')
- mix_bias_grad: float32 [3, 2048], P(None, 'seq')
- out_grad: float32 [2048, 2048], P('seq')
- gate_up_grad: float32 [2048, 2, 5632], P(None, None, 'seq')
- down_grad: float32 [5632, 2048], P('seq')
Inputs may be any that keep to these rules, and one draw needn't show every extreme that they name: `row_lengths`: rows 0 to 1 are 1024 long; every other row's length is a multiple of 128 and at most 256. `row_group`: each of rows 0 to 1 fills a group alone; every other group holds exactly three of the other rows.
All inputs are finite; a program needn't handle non-finite values.
Results may differ from a plain program's by a relative error of at most 0.02.
Values may be sent and summed in bfloat16 or wider, within the bound.
A program may use at most 320 MiB of HBM per device.

v0:
```python
import math
import jax
import jax.numpy as jnp
from jax import lax
from jax.sharding import PartitionSpec as P

HEAD_DIM = 64
ROT = 16
EPS = 1e-05
NEG = -1e30
BASE = 10000.0


def layer_norm(values, gain, bias):
    centered = values - jnp.mean(values, axis=-1, keepdims=True)
    scale = lax.rsqrt(jnp.mean(centered * centered, axis=-1, keepdims=True) + EPS)
    unit = centered * scale
    return (unit * gain + bias, unit, scale)


def norm_back(incoming, unit, scale, gain):
    along = incoming * gain
    inner = jnp.mean(along, axis=-1, keepdims=True)
    cross = jnp.mean(along * unit, axis=-1, keepdims=True)
    return (
        scale * (along - inner - unit * cross),
        jnp.sum(incoming * unit, axis=0),
        jnp.sum(incoming, axis=0),
    )


def rotate(values, where, sign):
    half = ROT // 2
    freq = BASE ** (-jnp.arange(half, dtype=jnp.float32) / half)
    angle = where.astype(jnp.float32)[:, None] * freq[None, :]
    cosine = jnp.cos(angle)[:, None, :]
    sine = sign * jnp.sin(angle)[:, None, :]
    first = values[..., :half]
    second = values[..., half:ROT]
    return jnp.concatenate(
        [first * cosine - second * sine, second * cosine + first * sine, values[..., ROT:]], axis=-1
    )


def unrotate(lowered, where):
    wide = lowered.astype(jnp.float32)
    turned = jnp.stack(
        [rotate(wide[:, 0], where, -1.0), rotate(wide[:, 1], where, -1.0), wide[:, 2]], axis=1
    )
    return turned.reshape(lowered.shape[0], 3, -1).astype(jnp.bfloat16)


def slot_rows(row_lengths, row_group, group, slots):
    order = jnp.arange(row_lengths.shape[0], dtype=jnp.int32)
    same = row_group == group
    earlier = (order[:, None] > order[None, :]) & same[None, :]
    begin = jnp.sum(jnp.where(earlier, row_lengths[None, :], 0), axis=1)
    finish = begin + row_lengths
    inside = same[None, :] & (slots[:, None] >= begin[None, :]) & (slots[:, None] < finish[None, :])
    label = jnp.sum(jnp.where(inside, order[None, :] + 1, 0), axis=1) - 1
    offset = jnp.sum(jnp.where(inside, slots[:, None] - begin[None, :], 0), axis=1)
    load = jnp.sum(jnp.where(same, row_lengths, 0))
    return (label, jnp.where(label < 0, slots - load, offset))


def block_scores(query, key, label, start, block):
    part = lax.dynamic_slice_in_dim(query, start, block, 0)
    rows = start + jnp.arange(block, dtype=jnp.int32)
    columns = jnp.arange(label.shape[0], dtype=jnp.int32)
    label_rows = lax.dynamic_slice_in_dim(label, start, block, 0)
    allowed = (label_rows[:, None] == label[None, :]) & (rows[:, None] >= columns[None, :])
    scores = jnp.einsum("qhe,khe->hqk", part, key, preferred_element_type=jnp.float32) * (
        1.0 / math.sqrt(query.shape[-1])
    )
    return (part, jnp.where(allowed[None], scores, NEG))


def attend(query, key, value, label, block):

    def one_block(index):
        part, scores = block_scores(query, key, label, index * block, block)
        top = jnp.max(scores, axis=-1, keepdims=True)
        weights = jnp.exp(scores - top)
        totals = jnp.sum(weights, axis=-1, keepdims=True)
        probs = (weights / totals).astype(jnp.bfloat16)
        mixed = jnp.einsum("hqk,khe->qhe", probs, value, preferred_element_type=jnp.float32)
        return (mixed, top[..., 0] + jnp.log(totals[..., 0]))

    mixed, log_totals = lax.map(one_block, jnp.arange(query.shape[0] // block, dtype=jnp.int32))
    return (mixed.reshape(query.shape), log_totals)


def attend_back(query, key, value, label, log_totals, mixed_back, block):
    scale = 1.0 / math.sqrt(query.shape[-1])

    def one_block(carry, index):
        key_back, value_back = carry
        start = index * block
        part, scores = block_scores(query, key, label, start, block)
        back_part = lax.dynamic_slice_in_dim(mixed_back, start, block, 0)
        probs = jnp.exp(scores - log_totals[index][..., None])
        value_back = value_back + jnp.einsum(
            "hqk,qhe->khe",
            probs.astype(jnp.bfloat16),
            back_part,
            preferred_element_type=jnp.float32,
        )
        probs_back = jnp.einsum(
            "qhe,khe->hqk", back_part, value, preferred_element_type=jnp.float32
        )
        inner = jnp.sum(probs_back * probs, axis=-1, keepdims=True)
        score_back = (probs * (probs_back - inner)).astype(jnp.bfloat16)
        query_back = (
            jnp.einsum("hqk,khe->qhe", score_back, key, preferred_element_type=jnp.float32) * scale
        )
        key_back = (
            key_back
            + jnp.einsum("hqk,qhe->khe", score_back, part, preferred_element_type=jnp.float32)
            * scale
        )
        return ((key_back, value_back), query_back)

    empty = jnp.zeros(key.shape, jnp.float32)
    (key_back, value_back), query_back = lax.scan(
        one_block, (empty, empty), jnp.arange(query.shape[0] // block, dtype=jnp.int32)
    )
    return (query_back.reshape(query.shape), key_back, value_back)


def silu_parts(gate_up):
    gate = gate_up[:, 0]
    upper = gate_up[:, 1]
    sigma = jax.nn.sigmoid(gate)
    return (gate * sigma * upper, gate, upper, sigma)


def gate_back(hidden_back, gate, upper, sigma):
    gate_part = hidden_back * upper * sigma * (1.0 + gate * (1.0 - sigma))
    up_part = hidden_back * gate * sigma
    return jnp.stack([gate_part, up_part], axis=1).astype(jnp.bfloat16)


def gather_rows(values):
    return lax.all_gather(values, "seq", axis=0, tiled=True)


def summed_rows(product, left):
    return lax.psum_scatter(
        product(left).astype(jnp.bfloat16), "seq", scatter_dimension=0, tiled=True
    ).astype(jnp.float32)


def on_device(
    tokens,
    norm_gains,
    norm_biases,
    mix_weight,
    mix_bias,
    out_weight,
    gate_up_weight,
    down_weight,
    row_lengths,
    row_group,
    cotangent,
):
    seq_count = lax.axis_size("seq")
    shard = lax.axis_index("seq")
    group = lax.axis_index("grp")
    slots_dev = tokens.shape[0]
    width = tokens.shape[1]
    group_slots = slots_dev * seq_count
    block = min(512, group_slots)
    local_width = width // seq_count
    local_heads = local_width // HEAD_DIM
    mine = shard * slots_dev + jnp.arange(slots_dev, dtype=jnp.int32)
    label_mine, place_mine = slot_rows(row_lengths, row_group, group, mine)
    label_all, place_all = slot_rows(
        row_lengths, row_group, group, jnp.arange(group_slots, dtype=jnp.int32)
    )
    inputs = tokens.astype(jnp.float32)
    upstream = cotangent.astype(jnp.float32) * (label_mine >= 0).astype(jnp.float32)[:, None]
    upstream_low = upstream.astype(jnp.bfloat16)
    normed, unit_one, scale_one = layer_norm(inputs, norm_gains[0], norm_biases[0])
    normed_low = normed.astype(jnp.bfloat16)
    mix_full, bias_full, out_full = (
        lax.all_gather(mix_weight, "seq", axis=2, tiled=True),
        lax.all_gather(mix_bias, "seq", axis=1, tiled=True),
        lax.all_gather(out_weight, "seq", axis=0, tiled=True),
    )
    mixin = jnp.einsum(
        "td,dcf->tcf", normed_low, mix_full, preferred_element_type=jnp.float32
    ) + bias_full.astype(jnp.float32)
    heads_in = mixin.reshape(slots_dev, 3, width // HEAD_DIM, HEAD_DIM)
    sending = jnp.stack(
        [
            rotate(heads_in[:, 0], place_mine, 1.0),
            rotate(heads_in[:, 1], place_mine, 1.0),
            heads_in[:, 2],
        ],
        axis=1,
    ).astype(jnp.bfloat16)
    arrived = lax.all_to_all(
        sending.reshape(slots_dev, 3, seq_count, local_width),
        "seq",
        split_axis=2,
        concat_axis=0,
        tiled=True,
    )
    arrived = arrived.reshape(group_slots, 3, local_heads, HEAD_DIM)
    query, key, value = (arrived[:, 0], arrived[:, 1], arrived[:, 2])
    mixed, log_totals = attend(query, key, value, label_all, block)
    attended = lax.all_to_all(
        mixed.reshape(group_slots, local_width).astype(jnp.bfloat16),
        "seq",
        split_axis=0,
        concat_axis=1,
        tiled=True,
    )
    resid = inputs + jnp.dot(attended, out_full, preferred_element_type=jnp.float32)
    normed_two, unit_two, scale_two = layer_norm(resid, norm_gains[1], norm_biases[1])
    normed_two_all = gather_rows(normed_two.astype(jnp.bfloat16))
    gate_up = jnp.einsum(
        "td,dcf->tcf", normed_two_all, gate_up_weight, preferred_element_type=jnp.float32
    )
    hidden, gate, upper, sigma = silu_parts(gate_up)
    hidden_low = hidden.astype(jnp.bfloat16)

    def down_product(part):
        return jnp.dot(part, down_weight, preferred_element_type=jnp.float32)

    layer_out = resid + summed_rows(down_product, hidden_low)
    upstream_all = gather_rows(upstream_low)
    down_shard = jnp.einsum(
        "tf,td->fd", hidden_low, upstream_all, preferred_element_type=jnp.float32
    )
    hidden_back = jnp.einsum(
        "td,fd->tf", upstream_all, down_weight, preferred_element_type=jnp.float32
    )
    gate_up_back = gate_back(hidden_back, gate, upper, sigma)
    gate_up_shard = jnp.einsum(
        "td,tcf->dcf", normed_two_all, gate_up_back, preferred_element_type=jnp.float32
    )

    def gate_up_product(part):
        return jnp.einsum("tcf,dcf->td", part, gate_up_weight, preferred_element_type=jnp.float32)

    normed_two_back = summed_rows(gate_up_product, gate_up_back)
    resid_part, gain_two, bias_two = norm_back(normed_two_back, unit_two, scale_two, norm_gains[1])
    resid_back = upstream + resid_part
    branch_low = resid_back.astype(jnp.bfloat16)
    out_term = jnp.einsum("te,td->ed", attended, branch_low, preferred_element_type=jnp.float32)
    attended_back = jnp.einsum(
        "td,ed->te", branch_low, out_full, preferred_element_type=jnp.float32
    ).astype(jnp.bfloat16)
    heads_back = lax.all_to_all(
        attended_back, "seq", split_axis=1, concat_axis=0, tiled=True
    ).reshape(group_slots, local_heads, HEAD_DIM)
    query_back, key_back, value_back = attend_back(
        query, key, value, label_all, log_totals, heads_back, block
    )
    lowered = (
        jnp.stack([query_back, key_back, value_back], axis=1)
        .astype(jnp.bfloat16)
        .reshape(group_slots, 3, 1, local_width)
    )
    returned = lax.all_to_all(lowered, "seq", split_axis=0, concat_axis=2, tiled=True).reshape(
        slots_dev, 3, width // HEAD_DIM, HEAD_DIM
    )
    mixin_back = unrotate(returned, place_mine)
    mix_term = jnp.einsum("td,tcf->dcf", normed_low, mixin_back, preferred_element_type=jnp.float32)
    bias_term = jnp.sum(mixin_back, axis=0, dtype=jnp.float32)
    normed_back = jnp.einsum(
        "tcf,dcf->td", mixin_back, mix_full, preferred_element_type=jnp.float32
    )
    mix_shard, bias_shard, out_shard = (
        lax.psum_scatter(
            mix_term.astype(jnp.bfloat16), "seq", scatter_dimension=2, tiled=True
        ).astype(jnp.float32),
        lax.psum_scatter(
            bias_term.astype(jnp.bfloat16), "seq", scatter_dimension=1, tiled=True
        ).astype(jnp.float32),
        lax.psum_scatter(
            out_term.astype(jnp.bfloat16), "seq", scatter_dimension=0, tiled=True
        ).astype(jnp.float32),
    )
    tokens_part, gain_one, bias_one = norm_back(normed_back, unit_one, scale_one, norm_gains[0])
    tokens_grad = (resid_back + tokens_part).astype(jnp.bfloat16)
    mix_grad, mix_bias_grad, out_grad, gate_up_grad, down_grad = (
        lax.psum(mix_shard.astype(jnp.bfloat16), "grp").astype(jnp.float32),
        lax.psum(bias_shard.astype(jnp.bfloat16), "grp").astype(jnp.float32),
        lax.psum(out_shard.astype(jnp.bfloat16), "grp").astype(jnp.float32),
        lax.psum(gate_up_shard.astype(jnp.bfloat16), "grp").astype(jnp.float32),
        lax.psum(down_shard.astype(jnp.bfloat16), "grp").astype(jnp.float32),
    )
    gains_grad, biases_grad = lax.psum(
        (jnp.stack([gain_one, gain_two]), jnp.stack([bias_one, bias_two])), ("grp", "seq")
    )
    return (
        layer_out.astype(jnp.bfloat16),
        tokens_grad,
        gains_grad,
        biases_grad,
        mix_grad,
        mix_bias_grad,
        out_grad,
        gate_up_grad,
        down_grad,
    )


def solution(mesh):
    placed = (
        P(("grp", "seq"), None),
        P(),
        P(),
        P(None, None, "seq"),
        P(None, "seq"),
        P("seq", None),
        P(None, None, "seq"),
        P("seq", None),
        P(),
        P(),
        P(("grp", "seq"), None),
    )
    return jax.shard_map(
        on_device,
        mesh=mesh,
        in_specs=placed,
        out_specs=(
            P(("grp", "seq"), None),
            P(("grp", "seq"), None),
            P(),
            P(),
            P(None, None, "seq"),
            P(None, "seq"),
            P("seq", None),
            P(None, None, "seq"),
            P("seq", None),
        ),
        check_vma=False,
    )
```

profile of v0, /device:TPU:0, one launch (start us, length us, event | category | flops | bytes accessed | tf_op | source)
XLA Modules:
  0.0 1248.3 jit_solution(738130817734868844)
XLA Ops:
  9.5 10.4 all_gather.16
  21.9 121.0 %all-gather.5.cloned.1.call-done = bf16[2048,3,2048]{2,0,1:T(8,128)(2,1)} async-done(((bf16[2048,3,256]{2,0,1:T(8,128)(2,1)}), bf16[2048,3,2048]{2,0,1:T(8,128)(2,1)}) %all-gather.5.cloned.1.call-update) | async-done | bytes 25165840 | tf_op jit(solution)/shard_map/all_gather | solution.py:186
  143.0 13.4 %convolution_add_fusion = f32[128,3,2048]{2,0,1:T(8,128)} fusion(bf16[2048,3,2048]{2,0,1:T(8,128)(2,1)} %all-gather.5.cloned.1.call-done, f32[3,2048]{1,0:T(4,128)S(1)} %convert_element_type.139, bf16[128,2048]{1,0:T(8,128)(2,1)S(1)} %copy-done.5, f32[2048]{0:T(1024)S(1)} %bitcast.195, f32[2048]{0:T(1024)S(1)} %bitcast.191, f32[128]{0:T(128)S(1)} %add_rsqrt_fusion.1, ...), kind=kOutput, calls=%fused_computation.63 | convolution fusion | flops 3223584768 | bytes 28877824 | tf_op jit(solution)/shard_map/td,dcf->tcf/dot_general | solution.py:190
  164.7 4.5 all-to-all-start
  169.3 35.6 %all-to-all-done = bf16[128,3,8,256]{0,3,1,2:T(8,128)(2,1)} async-done(((bf16[128,3,8,256]{0,3,1,2:T(8,128)(2,1)}), bf16[128,3,8,256]{0,3,1,2:T(8,128)(2,1)}, u32[]{:S(2)}, u32[]{:S(2)}) %all-to-all-start) | async-done | bytes 1572896 | tf_op jit(solution)/shard_map/all_to_all | solution.py:202
  215.6 21.5 %while.27 = (s32[]{:T(128)}, bf16[2,512,4,64]{1,3,2,0:T(8,128)(2,1)}, f32[2,4,512]{2,1,0:T(4,128)S(1)}, s32[2]{0:T(128)S(1)}, s32[1024]{0:T(1024)S(1)}, /*index=...) while((s32[]{:T(128)}, ...), condition=%wide.region_10.11_spmd, body=%wide.region_7.10_spmd.sunk | while | flops 563608064 | bytes 35469596 | solution.py:89
  243.5 4.2 all-to-all-start.1
  247.8 9.7 all-to-all-done.1
  257.4 4.9 fusion.81
  266.9 33.4 %all-gather.9.cloned.1.call-done = bf16[1024,2048]{1,0:T(8,128)(2,1)} async-done(((bf16[128,2048]{1,0:T(8,128)(2,1)}), bf16[1024,2048]{1,0:T(8,128)(2,1)}) %all-gather.9.cloned.1.call-update) | async-done | bytes 4194320 | tf_op jit(solution)/shard_map/all_gather | solution.py:144
  300.4 11.0 fusion.39
  311.4 28.1 %all-gather.11.cloned.1.call-done = bf16[1024,2048]{1,0:T(8,128)(2,1)} async-done(((bf16[128,2048]{1,0:T(8,128)(2,1)}), bf16[1024,2048]{1,0:T(8,128)(2,1)}) %all-gather.11.cloned.1.call-update) | async-done | bytes 4194320 | tf_op jit(solution)/shard_map/all_gather | solution.py:144
  339.5 8.3 fusion.45
  349.4 11.0 bitcast_convert_fusion
  360.4 6.4 convolution_convert_fusion.3
  366.9 45.0 %reduce-scatter.10.cloned.1.call-done = bf16[128,2048]{1,0:T(8,128)(2,1)} async-done(((bf16[1024,2048]{1,0:T(8,128)(2,1)}), bf16[128,2048]{1,0:T(8,128)(2,1)}) %reduce-scatter.10.cloned.1.call-update) | async-done | bytes 524304 | tf_op jit(solution)/shard_map/reduce_scatter | solution.py:148
  414.0 53.4 %reduce-scatter.8.cloned.1.call-done = bf16[128,2048]{1,0:T(8,128)(2,1)} async-done(((bf16[1024,2048]{1,0:T(8,128)(2,1)}), bf16[128,2048]{1,0:T(8,128)(2,1)}) %reduce-scatter.8.cloned.1.call-update) | async-done | bytes 524304 | tf_op jit(solution)/shard_map/reduce_scatter | solution.py:148
  469.7 7.1 convolution_convert_fusion.1
  476.8 6.3 convolution_convert_fusion.5
  487.7 9.4 all-to-all-done.2
  501.1 31.6 %while.28 = (s32[]{:T(128)}, f32[1024,4,64]{0,2,1:T(8,128)S(1)}, f32[1024,4,64]{0,2,1:T(8,128)}, bf16[2,512,4,64]{1,3,2,0:T(8,128)(2,1)}, s32[2]{0:T(128)S(1)}, ...) while((s32[]{:T(128)}, f32[1024,4,64]{0,2,1:T(8,128)S(1)}, ...), condition=%wide.region_19.20_spmd.clone, body=%wide.region_17.19_spmd.clone.sunk | while | flops 1376647680 | bytes 87103920 | solution.py:124
  540.5 29.5 %all_to_all.56 = bf16[1024,3,1,256]{3,1,2,0:T(4,128)(2,1)S(1)} all-to-all(bf16[1024,3,1,256]{3,1,2,0:T(4,128)(2,1)S(1)} %copy.98), channel_id=1, replica_groups=mesh['grp'=4,'seq'=8] {'seq'}, dimensions={0} | all-to-all | bytes 3145728 | tf_op jit(solution)/shard_map/all_to_all | solution.py:266
  578.5 12.0 convolution_convert_fusion
  590.6 10.8 convolution_convert_fusion.2
  603.1 8.9 convolution_convert_fusion.4
  612.0 134.7 %reduce-scatter.12.cloned.1.call-done = bf16[2048,3,256]{2,0,1:T(8,128)(2,1)} async-done(((bf16[2048,3,2048]{2,0,1:T(8,128)(2,1)}), bf16[2048,3,256]{2,0,1:T(8,128)(2,1)}) %reduce-scatter.12.cloned.1.call-update) | async-done | bytes 3145744 | tf_op jit(solution)/shard_map/reduce_scatter | solution.py:276
  746.7 14.6 %fusion.59 = (f32[2048]{0:T(1024)S(1)}, f32[128]{0:T(128)S(1)}, f32[128]{0:T(128)S(1)}, f32[2048]{0:T(1024)S(1)}, f32[128,2048]{1,0:T(8,128)}) fusion(bf16[128,2048]{1,0:T(8,128)(2,1)S(1)} %copy-done.6, f32[128]{0:T(128)S(1)} %copy-done.35, f32[128]{0:T(128)S(1)} %copy-done.33, f32[2048]{0:T(1024)S(1)} %bitcast.193, ...), kind=kOutput, calls=%fused_computation.93 | convolution fusion | flops 3225415680 | bytes 28338176 | tf_op jit(solution)/shard_map/tcf,dcf->td/dot_general | solution.py:272
  761.4 40.2 %all-reduce = (f32[2,2048]{1,0:T(2,128)}, f32[2,2048]{1,0:T(2,128)}) all-reduce(f32[2,2048]{1,0:T(2,128)S(1)} %pad_maximum_fusion.10, f32[2,2048]{1,0:T(2,128)S(1)} %pad_maximum_fusion.11), channel_id=1, replica_groups=mesh['grp'=4,'seq'=8] {'grp','seq'}, use_global_device_ids=true, to_apply=%region_24.25 | all-reduce | flops 8192 | bytes 65536 | tf_op jit(solution)/shard_map/psum | solution.py:295
  805.0 12.3 psum.52
  817.9 407.1 %all-reduce.4.cloned.1.call-done = (bf16[2048,3,256]{2,0,1:T(8,128)(2,1)}, bf16[256,2048]{1,0:T(8,128)(2,1)}, bf16[2048,2,704]{0,2,1:T(8,128)(2,1)}, bf16[704,2048]{1,0:T(8,128)(2,1)}) async-done(((bf16[2048,3,256]{2,0,1:T(8,128)(2,1)}, bf16[256,2048]{1,0:T(8,128)(2,1)}, bf16[2048,2,704]{0,2,1:T(8,128)(2,1)}, bf16[704,2048]{1,0:T(8,128)(2,1)}), (bf16[2048,3,256]{2,0,1:T(8,128)(2,1)}, ...) | async-done | bytes 12845072 | tf_op jit(solution)/shard_map/psum | solution.py:289
  1228.0 3.7 convert_element_type.161
  1235.0 6.0 convert_element_type.166
  (248 shorter events, 123.5 us)
Async XLA Ops:
  7.2 332.3 %copy-start = (bf16[704,2048]{1,0:T(8,128)(2,1)S(1)}, bf16[704,2048]{1,0:T(8,128)(2,1)}, u32[]{:S(2)}) copy-start(bf16[704,2048]{1,0:T(8,128)(2,1)} %param.22) | copy-start | bytes 8650756
  7.2 12.8 %copy-start.5 = (bf16[128,2048]{1,0:T(8,128)(2,1)S(1)}, bf16[128,2048]{1,0:T(8,128)(2,1)}, u32[]{:S(2)}) copy-start(bf16[128,2048]{1,0:T(8,128)(2,1)} %param.15) | copy-start | bytes 1572868
  7.2 14.6 %copy-start.30 = (f32[2,2048]{1,0:T(2,128)S(1)}, f32[2,2048]{1,0:T(2,128)}, u32[]{:S(2)}) copy-start(f32[2,2048]{1,0:T(2,128)} %param.16) | copy-start | bytes 49156
  7.2 14.6 %copy-start.31 = (f32[2,2048]{1,0:T(2,128)S(1)}, f32[2,2048]{1,0:T(2,128)}, u32[]{:S(2)}) copy-start(f32[2,2048]{1,0:T(2,128)} %param.17) | copy-start | bytes 49156
  7.3 135.7 %all-gather.5.cloned.1.call-start = ((), (), s32[]{:S(2)}) async-start(), calls=%async_computation.9 | async-start | bytes 28311552 | tf_op jit(solution)/shard_map/all_gather | solution.py:186
  8.0 239.8 %all-gather.7.cloned.1.call-start = ((), (), s32[]{:S(2)}) async-start(), calls=%async_computation.10 | async-start | bytes 9437184 | tf_op jit(solution)/shard_map/all_gather | solution.py:188
  20.2 136.2 %copy-start.32 = (f32[128]{0:T(128)}, f32[128]{0:T(128)S(1)}, u32[]{:S(2)}) copy-start(f32[128]{0:T(128)S(1)} %broadcast_multiply_fusion.6) | copy-start | bytes 1540
  20.5 135.9 %copy-start.34 = (f32[128]{0:T(128)}, f32[128]{0:T(128)S(1)}, u32[]{:S(2)}) copy-start(f32[128]{0:T(128)S(1)} %add_rsqrt_fusion.1) | copy-start | bytes 1540
  21.9 141.2 %copy-start.25 = (f32[128,8]{0,1:T(8,128)}, f32[128,8]{0,1:T(8,128)S(1)}, u32[]{:S(2)}) copy-start(f32[128,8]{0,1:T(8,128)S(1)} %get-tuple-element.253) | copy-start | bytes 12292
  21.9 134.5 %copy-start.21 = (f32[1,2048]{1,0:T(1,128)}, f32[1,2048]{1,0:T(1,128)S(1)}, u32[]{:S(2)}) copy-start(f32[1,2048]{1,0:T(1,128)S(1)} %get-tuple-element.244) | copy-start | bytes 24580
  21.9 134.4 %copy-start.23 = (f32[1,2048]{1,0:T(1,128)}, f32[1,2048]{1,0:T(1,128)S(1)}, u32[]{:S(2)}) copy-start(f32[1,2048]{1,0:T(1,128)S(1)} %get-tuple-element.246) | copy-start | bytes 24580
  164.7 40.2 %all-to-all-start = ((bf16[128,3,8,256]{0,3,1,2:T(8,128)(2,1)}), bf16[128,3,8,256]{0,3,1,2:T(8,128)(2,1)}, u32[]{:S(2)}, u32[]{:S(2)}) async-start(bf16[128,3,8,256]{0,3,1,2:T(8,128)(2,1)} %copy.91), calls=%async_computation | async-start | bytes 3145728 | tf_op jit(solution)/shard_map/all_to_all | solution.py:202
  243.5 13.9 %all-to-all-start.1 = ((bf16[8,128,256]{1,2,0:T(8,128)(2,1)}), bf16[8,128,256]{1,2,0:T(8,128)(2,1)}, u32[]{:S(2)}, u32[]{:S(2)}) async-start(bf16[8,128,256]{1,2,0:T(8,128)(2,1)} %copy.94), calls=%async_computation.1 | async-start | bytes 1048576 | tf_op jit(solution)/shard_map/all_to_all | solution.py:212
  247.7 52.7 %all-gather.9.cloned.1.call-start = ((), (), s32[]{:S(2)}) async-start(), calls=%async_computation.11 | async-start | bytes 4718592 | tf_op jit(solution)/shard_map/all_gather | solution.py:144
  264.4 75.0 %all-gather.11.cloned.1.call-start = ((), (), s32[]{:S(2)}) async-start(), calls=%async_computation.13 | async-start | bytes 4718592 | tf_op jit(solution)/shard_map/all_gather | solution.py:144
  266.5 145.4 %reduce-scatter.10.cloned.1.call-start = ((), (), s32[]{:S(2)}) async-start(), calls=%async_computation.14 | async-start | bytes 4718592 | tf_op jit(solution)/shard_map/reduce_scatter | solution.py:148
  360.4 107.0 %reduce-scatter.8.cloned.1.call-start = ((), (), s32[]{:S(2)}) async-start(), calls=%async_computation.12 | async-start | bytes 4718592 | tf_op jit(solution)/shard_map/reduce_scatter | solution.py:148
  366.8 45.0 %copy-start.4 = (f32[128,2048]{1,0:T(8,128)S(1)}, f32[128,2048]{1,0:T(8,128)}, u32[]{:S(2)}) copy-start(f32[128,2048]{1,0:T(8,128)} %copy-done.3) | copy-start | bytes 3145732
  366.8 100.5 %copy-start.18 = (bf16[128,2048]{1,0:T(8,128)(2,1)S(1)}, bf16[128,2048]{1,0:T(8,128)(2,1)}, u32[]{:S(2)}) copy-start(bf16[128,2048]{1,0:T(8,128)(2,1)} %param.25) | copy-start | bytes 1572868
  366.9 245.1 %reduce-scatter.14.cloned.1.call-start = ((), (), s32[]{:S(2)}) async-start(), calls=%async_computation.16 | async-start | bytes 9437184 | tf_op jit(solution)/shard_map/reduce_scatter | solution.py:282
  469.7 7.2 copy-start.9
  483.1 18.0 %copy-start.2 = (bf16[1024,4,64]{0,2,1:T(8,128)(2,1)S(1)}, bf16[1024,4,64]{0,2,1:T(8,128)(2,1)}, u32[]{:S(2)}) copy-start(bf16[1024,4,64]{0,2,1:T(8,128)(2,1)} %get-tuple-element.490) | copy-start | bytes 1572868
  483.1 18.0 %copy-start.8 = (bf16[1024,4,64]{0,2,1:T(8,128)(2,1)S(1)}, bf16[1024,4,64]{0,2,1:T(8,128)(2,1)}, u32[]{:S(2)}) copy-start(bf16[1024,4,64]{0,2,1:T(8,128)(2,1)} %get-tuple-element.491) | copy-start | bytes 1572868
  484.0 13.2 %all-to-all-start.2 = ((bf16[128,8,256]{2,0,1:T(8,128)(2,1)}), bf16[128,8,256]{2,0,1:T(8,128)(2,1)S(1)}, u32[]{:S(2)}, u32[]{:S(2)}) async-start(bf16[128,8,256]{2,0,1:T(8,128)(2,1)} %bitcast.142), calls=%async_computation.4 | async-start | bytes 1048576 | tf_op jit(solution)/shard_map/all_to_all | solution.py:255
  487.5 259.2 %reduce-scatter.12.cloned.1.call-start = ((), (), s32[]{:S(2)}) async-start(), calls=%async_computation.15 | async-start | bytes 28311552 | tf_op jit(solution)/shard_map/reduce_scatter | solution.py:276
  590.5 213.5 %reduce-scatter.16.cloned.1.call-start = ((), (), s32[]{:S(2)}) async-start(), calls=%async_computation.17 | async-start | bytes 589824
  602.8 622.3 %all-reduce.4.cloned.1.call-start = ((), (), s32[]{:S(2)}) async-start(), calls=%async_computation.18 | async-start | bytes 25690112 | tf_op jit(solution)/shard_map/psum | solution.py:289
  746.7 14.7 %copy-start.28 = (f32[2048]{0:T(1024)S(1)}, f32[2048]{0:T(1024)}, u32[]{:S(2)}) copy-start(f32[2048]{0:T(1024)} %get-tuple-element.165) | copy-start | bytes 24580
  746.7 14.7 %copy-start.27 = (f32[2048]{0:T(1024)S(1)}, f32[2048]{0:T(1024)}, u32[]{:S(2)}) copy-start(f32[2048]{0:T(1024)} %get-tuple-element.170) | copy-start | bytes 24580
  746.7 54.9 %copy-start.10 = (f32[128,2048]{1,0:T(8,128)S(1)}, f32[128,2048]{1,0:T(8,128)}, u32[]{:S(2)}) copy-start(f32[128,2048]{1,0:T(8,128)} %copy-done.9) | copy-start | bytes 3145732
  1225.0 10.0 slice-start
  1228.0 7.1 slice-start.1
  (32 other events, 60.9 us)
Sparse Core Ops, SparseCore 0:
  10.0 132.9 all-gather.4
  144.9 68.7 all-gather.6
  264.5 35.7 all-gather.8
  302.7 36.7 all-gather.10
  360.5 51.3 reduce-scatter.9
  416.0 51.2 reduce-scatter.7
  476.9 71.4 reduce-scatter.13
  590.6 155.9 reduce-scatter.11
  750.0 34.2 reduce-scatter.15
  788.2 436.8 all-reduce.3
where the time goes:
time: 1250 us
  waiting for transfers between devices  879 us (70%)
  matrix products  145 us (12%)
  blocking collectives  92.4 us (7%)
  local copies, waits for them, and re-layouts  49.7 us (4%)
  other arithmetic  47.1 us (4%)
  between operations  15.2 us (1%)
  starting transfers between devices  13.4 us (1%)
    psum x1, waiting for transfers between devices, on_device(): lax.psum(mix_shard.astype(jnp.bfloat16), 'grp').astype(jnp.float32)  407 us
    reduce_scatter x1, waiting for transfers between devices, on_device(): lax.psum_scatter(mix_term.astype(jnp.bfloat16), 'seq', scatter_dimension=...  135 us
    all_gather x1, waiting for transfers between devices, on_device(): lax.all_gather(mix_weight, 'seq', axis=2, tiled=True)  121 us
    reduce_scatter x2, waiting for transfers between devices, summed_rows(): lax.psum_scatter(product(left).astype(jnp.bfloat16), 'seq', scatter_dimen...  98.3 us
    all_gather x2, waiting for transfers between devices, gather_rows(): return lax.all_gather(values, 'seq', axis=0, tiled=True)  61.5 us
    psum x1, blocking collectives, on_device(): lax.psum((jnp.stack([gain_one, gain_two]), jnp.stack([bias_one, bias_two]...  40.2 us
    all_to_all x1, waiting for transfers between devices, on_device(): lax.all_to_all(sending.reshape(slots_dev, 3, seq_count, local_width), 'se...  35.6 us
    all_to_all x1, blocking collectives, on_device(): lax.all_to_all(lowered, 'seq', split_axis=0, concat_axis=2, tiled=True)  29.5 us
  transfers between devices with their start and end apart: 13, of which 10 were waited for; matrix products, arithmetic and copies ran while one was open for 15% of the time, Pallas kernels for 0%

commit v1 on v0

--- a/solution.py
+++ b/solution.py
@@ -293,7 +293,7 @@
         lax.psum(down_shard.astype(jnp.bfloat16), "grp").astype(jnp.float32),
     )
     gains_grad, biases_grad = lax.psum(
-        (jnp.stack([gain_one, gain_two]), jnp.stack([bias_one, bias_two])), ("grp", "seq")
+        lax.psum((jnp.stack([gain_one, gain_two]), jnp.stack([bias_one, bias_two])), "seq"), "grp"
     )
     return (
         layer_out.astype(jnp.bfloat16),

time: 1250 us -> 1250 us (level)
    psum x0 -> x1, blocking collectives: none -> 20.2 us  [on_device(): lax.psum(lax.psum((jnp.stack([gain_one, gain_two]), jnp.stack([bias_one,...]
    psum x1, blocking collectives: 40.2 us -> 23.1 us  [on_device(): lax.psum((jnp.stack([gain_one, gain_two]), jnp.stack([bias_one, bias_two]...]
where the time goes in v1:
time: 1250 us
  waiting for transfers between devices  877 us (70%)
  matrix products  145 us (12%)
  blocking collectives  94.3 us (8%)
  local copies, waits for them, and re-layouts  49.8 us (4%)
  other arithmetic  47.1 us (4%)
  between operations  15.2 us (1%)
  starting transfers between devices  13.4 us (1%)
    psum x1, waiting for transfers between devices, on_device(): lax.psum(mix_shard.astype(jnp.bfloat16), 'grp').astype(jnp.float32)  405 us
    reduce_scatter x1, waiting for transfers between devices, on_device(): lax.psum_scatter(mix_term.astype(jnp.bfloat16), 'seq', scatter_dimension=...  135 us
    all_gather x1, waiting for transfers between devices, on_device(): lax.all_gather(mix_weight, 'seq', axis=2, tiled=True)  121 us
    reduce_scatter x2, waiting for transfers between devices, summed_rows(): lax.psum_scatter(product(left).astype(jnp.bfloat16), 'seq', scatter_dimen...  98.3 us
    all_gather x2, waiting for transfers between devices, gather_rows(): return lax.all_gather(values, 'seq', axis=0, tiled=True)  61.5 us
    all_to_all x1, waiting for transfers between devices, on_device(): lax.all_to_all(sending.reshape(slots_dev, 3, seq_count, local_width), 'se...  35.6 us
    all_to_all x1, blocking collectives, on_device(): lax.all_to_all(lowered, 'seq', split_axis=0, concat_axis=2, tiled=True)  29.3 us
  transfers between devices with their start and end apart: 13, of which 10 were waited for; matrix products, arithmetic and copies ran while one was open for 15% of the time, Pallas kernels for 0%

profile of v1, /device:TPU:0, one launch (start us, length us, event | category | flops | bytes accessed | tf_op | source)
XLA Modules:
  0.0 1248.6 jit_solution(2970910060220202975)
XLA Ops:
  9.5 10.4 all_gather.16
  21.9 121.0 %all-gather.5.cloned.1.call-done = bf16[2048,3,2048]{2,0,1:T(8,128)(2,1)} async-done(((bf16[2048,3,256]{2,0,1:T(8,128)(2,1)}), bf16[2048,3,2048]{2,0,1:T(8,128)(2,1)}) %all-gather.5.cloned.1.call-update) | async-done | bytes 25165840 | tf_op jit(solution)/shard_map/all_gather | solution.py:186
  143.0 13.4 %convolution_add_fusion = f32[128,3,2048]{2,0,1:T(8,128)} fusion(bf16[2048,3,2048]{2,0,1:T(8,128)(2,1)} %all-gather.5.cloned.1.call-done, f32[3,2048]{1,0:T(4,128)S(1)} %convert_element_type.139, bf16[128,2048]{1,0:T(8,128)(2,1)S(1)} %copy-done.5, f32[2048]{0:T(1024)S(1)} %bitcast.195, f32[2048]{0:T(1024)S(1)} %bitcast.191, f32[128]{0:T(128)S(1)} %add_rsqrt_fusion.1, ...), kind=kOutput, calls=%fused_computation.63 | convolution fusion | flops 3223584768 | bytes 28877824 | tf_op jit(solution)/shard_map/td,dcf->tcf/dot_general | solution.py:190
  164.7 4.5 all-to-all-start
  169.3 35.6 %all-to-all-done = bf16[128,3,8,256]{0,3,1,2:T(8,128)(2,1)} async-done(((bf16[128,3,8,256]{0,3,1,2:T(8,128)(2,1)}), bf16[128,3,8,256]{0,3,1,2:T(8,128)(2,1)}, u32[]{:S(2)}, u32[]{:S(2)}) %all-to-all-start) | async-done | bytes 1572896 | tf_op jit(solution)/shard_map/all_to_all | solution.py:202
  215.6 21.5 %while.27 = (s32[]{:T(128)}, bf16[2,512,4,64]{1,3,2,0:T(8,128)(2,1)}, f32[2,4,512]{2,1,0:T(4,128)S(1)}, s32[2]{0:T(128)S(1)}, s32[1024]{0:T(1024)S(1)}, /*index=...) while((s32[]{:T(128)}, ...), condition=%wide.region_10.11_spmd, body=%wide.region_7.10_spmd.sunk | while | flops 563608064 | bytes 35469596 | solution.py:89
  243.5 4.2 all-to-all-start.1
  247.8 9.7 all-to-all-done.1
  257.5 4.9 fusion.81
  267.0 33.4 %all-gather.9.cloned.1.call-done = bf16[1024,2048]{1,0:T(8,128)(2,1)} async-done(((bf16[128,2048]{1,0:T(8,128)(2,1)}), bf16[1024,2048]{1,0:T(8,128)(2,1)}) %all-gather.9.cloned.1.call-update) | async-done | bytes 4194320 | tf_op jit(solution)/shard_map/all_gather | solution.py:144
  300.4 11.0 fusion.39
  311.4 28.1 %all-gather.11.cloned.1.call-done = bf16[1024,2048]{1,0:T(8,128)(2,1)} async-done(((bf16[128,2048]{1,0:T(8,128)(2,1)}), bf16[1024,2048]{1,0:T(8,128)(2,1)}) %all-gather.11.cloned.1.call-update) | async-done | bytes 4194320 | tf_op jit(solution)/shard_map/all_gather | solution.py:144
  339.5 8.3 fusion.45
  349.4 11.0 bitcast_convert_fusion
  360.5 6.4 convolution_convert_fusion.3
  366.9 45.0 %reduce-scatter.10.cloned.1.call-done = bf16[128,2048]{1,0:T(8,128)(2,1)} async-done(((bf16[1024,2048]{1,0:T(8,128)(2,1)}), bf16[128,2048]{1,0:T(8,128)(2,1)}) %reduce-scatter.10.cloned.1.call-update) | async-done | bytes 524304 | tf_op jit(solution)/shard_map/reduce_scatter | solution.py:148
  414.0 53.4 %reduce-scatter.8.cloned.1.call-done = bf16[128,2048]{1,0:T(8,128)(2,1)} async-done(((bf16[1024,2048]{1,0:T(8,128)(2,1)}), bf16[128,2048]{1,0:T(8,128)(2,1)}) %reduce-scatter.8.cloned.1.call-update) | async-done | bytes 524304 | tf_op jit(solution)/shard_map/reduce_scatter | solution.py:148
  469.7 7.1 convolution_convert_fusion.1
  476.9 6.3 convolution_convert_fusion.5
  487.7 9.4 all-to-all-done.2
  501.1 32.1 %while.28 = (s32[]{:T(128)}, f32[1024,4,64]{0,2,1:T(8,128)S(1)}, f32[1024,4,64]{0,2,1:T(8,128)}, bf16[2,512,4,64]{1,3,2,0:T(8,128)(2,1)}, s32[2]{0:T(128)S(1)}, ...) while((s32[]{:T(128)}, f32[1024,4,64]{0,2,1:T(8,128)S(1)}, ...), condition=%wide.region_19.20_spmd.clone, body=%wide.region_17.19_spmd.clone.sunk | while | flops 1376647680 | bytes 87103920 | solution.py:124
  541.0 29.3 %all_to_all.56 = bf16[1024,3,1,256]{3,1,2,0:T(4,128)(2,1)S(1)} all-to-all(bf16[1024,3,1,256]{3,1,2,0:T(4,128)(2,1)S(1)} %copy.98), channel_id=1, replica_groups=mesh['grp'=4,'seq'=8] {'seq'}, dimensions={0} | all-to-all | bytes 3145728 | tf_op jit(solution)/shard_map/all_to_all | solution.py:266
  578.7 12.0 convolution_convert_fusion
  590.7 10.8 convolution_convert_fusion.2
  603.2 8.9 convolution_convert_fusion.4
  612.1 134.8 %reduce-scatter.12.cloned.1.call-done = bf16[2048,3,256]{2,0,1:T(8,128)(2,1)} async-done(((bf16[2048,3,2048]{2,0,1:T(8,128)(2,1)}), bf16[2048,3,256]{2,0,1:T(8,128)(2,1)}) %reduce-scatter.12.cloned.1.call-update) | async-done | bytes 3145744 | tf_op jit(solution)/shard_map/reduce_scatter | solution.py:276
  746.9 14.6 %fusion.59 = (f32[2048]{0:T(1024)S(1)}, f32[128]{0:T(128)S(1)}, f32[128]{0:T(128)S(1)}, f32[2048]{0:T(1024)S(1)}, f32[128,2048]{1,0:T(8,128)}) fusion(bf16[128,2048]{1,0:T(8,128)(2,1)S(1)} %copy-done.6, f32[128]{0:T(128)S(1)} %copy-done.35, f32[128]{0:T(128)S(1)} %copy-done.33, f32[2048]{0:T(1024)S(1)} %bitcast.193, ...), kind=kOutput, calls=%fused_computation.93 | convolution fusion | flops 3225415680 | bytes 28338176 | tf_op jit(solution)/shard_map/tcf,dcf->td/dot_general | solution.py:272
  761.6 23.1 %all-reduce = (f32[2,2048]{1,0:T(2,128)S(1)}, f32[2,2048]{1,0:T(2,128)S(1)}) all-reduce(f32[2,2048]{1,0:T(2,128)S(1)} %pad_maximum_fusion.10, f32[2,2048]{1,0:T(2,128)S(1)} %pad_maximum_fusion.11), channel_id=1, replica_groups=mesh['grp'=4,'seq'=8] {'seq'}, use_global_device_ids=true, to_apply=%region_24.25 | all-reduce | flops 8192 | bytes 65536 | tf_op jit(solution)/shard_map/psum | solution.py:296
  784.7 20.2 %all-reduce.1 = (f32[2,2048]{1,0:T(2,128)}, f32[2,2048]{1,0:T(2,128)}) all-reduce(f32[2,2048]{1,0:T(2,128)S(1)} %get-tuple-element.211, f32[2,2048]{1,0:T(2,128)S(1)} %get-tuple-element.212), channel_id=1, replica_groups=mesh['grp'=4,'seq'=8] {'grp'}, use_global_device_ids=true, to_apply=%region_25.26 | all-reduce | flops 8192 | bytes 65536 | tf_op jit(solution)/shard_map/psum | solution.py:295
  808.3 11.3 psum.68
  820.3 405.0 %all-reduce.5.cloned.1.call-done = (bf16[2048,3,256]{2,0,1:T(8,128)(2,1)}, bf16[256,2048]{1,0:T(8,128)(2,1)}, bf16[2048,2,704]{0,2,1:T(8,128)(2,1)}, bf16[704,2048]{1,0:T(8,128)(2,1)}) async-done(((bf16[2048,3,256]{2,0,1:T(8,128)(2,1)}, bf16[256,2048]{1,0:T(8,128)(2,1)}, bf16[2048,2,704]{0,2,1:T(8,128)(2,1)}, bf16[704,2048]{1,0:T(8,128)(2,1)}), (bf16[2048,3,256]{2,0,1:T(8,128)(2,1)}, ...) | async-done | bytes 12845072 | tf_op jit(solution)/shard_map/psum | solution.py:289
  1235.3 6.0 convert_element_type.166
  (249 shorter events, 127.3 us)
Async XLA Ops:
  7.2 332.3 %copy-start = (bf16[704,2048]{1,0:T(8,128)(2,1)S(1)}, bf16[704,2048]{1,0:T(8,128)(2,1)}, u32[]{:S(2)}) copy-start(bf16[704,2048]{1,0:T(8,128)(2,1)} %param.22) | copy-start | bytes 8650756
  7.2 12.8 %copy-start.5 = (bf16[128,2048]{1,0:T(8,128)(2,1)S(1)}, bf16[128,2048]{1,0:T(8,128)(2,1)}, u32[]{:S(2)}) copy-start(bf16[128,2048]{1,0:T(8,128)(2,1)} %param.15) | copy-start | bytes 1572868
  7.2 14.6 %copy-start.30 = (f32[2,2048]{1,0:T(2,128)S(1)}, f32[2,2048]{1,0:T(2,128)}, u32[]{:S(2)}) copy-start(f32[2,2048]{1,0:T(2,128)} %param.16) | copy-start | bytes 49156
  7.2 14.6 %copy-start.31 = (f32[2,2048]{1,0:T(2,128)S(1)}, f32[2,2048]{1,0:T(2,128)}, u32[]{:S(2)}) copy-start(f32[2,2048]{1,0:T(2,128)} %param.17) | copy-start | bytes 49156
  7.3 135.7 %all-gather.5.cloned.1.call-start = ((), (), s32[]{:S(2)}) async-start(), calls=%async_computation.9 | async-start | bytes 28311552 | tf_op jit(solution)/shard_map/all_gather | solution.py:186
  8.0 239.8 %all-gather.7.cloned.1.call-start = ((), (), s32[]{:S(2)}) async-start(), calls=%async_computation.10 | async-start | bytes 9437184 | tf_op jit(solution)/shard_map/all_gather | solution.py:188
  20.2 136.2 %copy-start.32 = (f32[128]{0:T(128)}, f32[128]{0:T(128)S(1)}, u32[]{:S(2)}) copy-start(f32[128]{0:T(128)S(1)} %broadcast_multiply_fusion.6) | copy-start | bytes 1540
  20.5 135.9 %copy-start.34 = (f32[128]{0:T(128)}, f32[128]{0:T(128)S(1)}, u32[]{:S(2)}) copy-start(f32[128]{0:T(128)S(1)} %add_rsqrt_fusion.1) | copy-start | bytes 1540
  21.9 141.2 %copy-start.25 = (f32[128,8]{0,1:T(8,128)}, f32[128,8]{0,1:T(8,128)S(1)}, u32[]{:S(2)}) copy-start(f32[128,8]{0,1:T(8,128)S(1)} %get-tuple-element.255) | copy-start | bytes 12292
  21.9 134.5 %copy-start.21 = (f32[1,2048]{1,0:T(1,128)}, f32[1,2048]{1,0:T(1,128)S(1)}, u32[]{:S(2)}) copy-start(f32[1,2048]{1,0:T(1,128)S(1)} %get-tuple-element.246) | copy-start | bytes 24580
  21.9 134.4 %copy-start.23 = (f32[1,2048]{1,0:T(1,128)}, f32[1,2048]{1,0:T(1,128)S(1)}, u32[]{:S(2)}) copy-start(f32[1,2048]{1,0:T(1,128)S(1)} %get-tuple-element.248) | copy-start | bytes 24580
  164.7 40.2 %all-to-all-start = ((bf16[128,3,8,256]{0,3,1,2:T(8,128)(2,1)}), bf16[128,3,8,256]{0,3,1,2:T(8,128)(2,1)}, u32[]{:S(2)}, u32[]{:S(2)}) async-start(bf16[128,3,8,256]{0,3,1,2:T(8,128)(2,1)} %copy.91), calls=%async_computation | async-start | bytes 3145728 | tf_op jit(solution)/shard_map/all_to_all | solution.py:202
  243.5 13.9 %all-to-all-start.1 = ((bf16[8,128,256]{1,2,0:T(8,128)(2,1)}), bf16[8,128,256]{1,2,0:T(8,128)(2,1)}, u32[]{:S(2)}, u32[]{:S(2)}) async-start(bf16[8,128,256]{1,2,0:T(8,128)(2,1)} %copy.94), calls=%async_computation.1 | async-start | bytes 1048576 | tf_op jit(solution)/shard_map/all_to_all | solution.py:212
  247.7 52.7 %all-gather.9.cloned.1.call-start = ((), (), s32[]{:S(2)}) async-start(), calls=%async_computation.11 | async-start | bytes 4718592 | tf_op jit(solution)/shard_map/all_gather | solution.py:144
  264.4 75.0 %all-gather.11.cloned.1.call-start = ((), (), s32[]{:S(2)}) async-start(), calls=%async_computation.13 | async-start | bytes 4718592 | tf_op jit(solution)/shard_map/all_gather | solution.py:144
  266.5 145.4 %reduce-scatter.10.cloned.1.call-start = ((), (), s32[]{:S(2)}) async-start(), calls=%async_computation.14 | async-start | bytes 4718592 | tf_op jit(solution)/shard_map/reduce_scatter | solution.py:148
  360.4 107.0 %reduce-scatter.8.cloned.1.call-start = ((), (), s32[]{:S(2)}) async-start(), calls=%async_computation.12 | async-start | bytes 4718592 | tf_op jit(solution)/shard_map/reduce_scatter | solution.py:148
  366.8 45.0 %copy-start.4 = (f32[128,2048]{1,0:T(8,128)S(1)}, f32[128,2048]{1,0:T(8,128)}, u32[]{:S(2)}) copy-start(f32[128,2048]{1,0:T(8,128)} %copy-done.3) | copy-start | bytes 3145732
  366.9 100.5 %copy-start.18 = (bf16[128,2048]{1,0:T(8,128)(2,1)S(1)}, bf16[128,2048]{1,0:T(8,128)(2,1)}, u32[]{:S(2)}) copy-start(bf16[128,2048]{1,0:T(8,128)(2,1)} %param.25) | copy-start | bytes 1572868
  366.9 245.2 %reduce-scatter.14.cloned.1.call-start = ((), (), s32[]{:S(2)}) async-start(), calls=%async_computation.16 | async-start | bytes 9437184 | tf_op jit(solution)/shard_map/reduce_scatter | solution.py:282
  469.7 7.1 copy-start.9
  483.1 18.0 %copy-start.2 = (bf16[1024,4,64]{0,2,1:T(8,128)(2,1)S(1)}, bf16[1024,4,64]{0,2,1:T(8,128)(2,1)}, u32[]{:S(2)}) copy-start(bf16[1024,4,64]{0,2,1:T(8,128)(2,1)} %get-tuple-element.492) | copy-start | bytes 1572868
  483.1 18.0 %copy-start.8 = (bf16[1024,4,64]{0,2,1:T(8,128)(2,1)S(1)}, bf16[1024,4,64]{0,2,1:T(8,128)(2,1)}, u32[]{:S(2)}) copy-start(bf16[1024,4,64]{0,2,1:T(8,128)(2,1)} %get-tuple-element.493) | copy-start | bytes 1572868
  484.0 13.2 %all-to-all-start.2 = ((bf16[128,8,256]{2,0,1:T(8,128)(2,1)}), bf16[128,8,256]{2,0,1:T(8,128)(2,1)S(1)}, u32[]{:S(2)}, u32[]{:S(2)}) async-start(bf16[128,8,256]{2,0,1:T(8,128)(2,1)} %bitcast.142), calls=%async_computation.4 | async-start | bytes 1048576 | tf_op jit(solution)/shard_map/all_to_all | solution.py:255
  487.5 259.4 %reduce-scatter.12.cloned.1.call-start = ((), (), s32[]{:S(2)}) async-start(), calls=%async_computation.15 | async-start | bytes 28311552 | tf_op jit(solution)/shard_map/reduce_scatter | solution.py:276
  590.7 216.7 %reduce-scatter.16.cloned.1.call-start = ((), (), s32[]{:S(2)}) async-start(), calls=%async_computation.17 | async-start | bytes 589824
  602.9 622.4 %all-reduce.5.cloned.1.call-start = ((), (), s32[]{:S(2)}) async-start(), calls=%async_computation.18 | async-start | bytes 25690112 | tf_op jit(solution)/shard_map/psum | solution.py:289
  746.9 14.7 %copy-start.28 = (f32[2048]{0:T(1024)S(1)}, f32[2048]{0:T(1024)}, u32[]{:S(2)}) copy-start(f32[2048]{0:T(1024)} %get-tuple-element.165) | copy-start | bytes 24580
  746.9 14.7 %copy-start.27 = (f32[2048]{0:T(1024)S(1)}, f32[2048]{0:T(1024)}, u32[]{:S(2)}) copy-start(f32[2048]{0:T(1024)} %get-tuple-element.170) | copy-start | bytes 24580
  746.9 58.0 %copy-start.10 = (f32[128,2048]{1,0:T(8,128)S(1)}, f32[128,2048]{1,0:T(8,128)}, u32[]{:S(2)}) copy-start(f32[128,2048]{1,0:T(8,128)} %copy-done.9) | copy-start | bytes 3145732
  1225.3 10.0 slice-start
  1228.2 7.1 slice-start.1
  (32 other events, 60.9 us)
Sparse Core Ops, SparseCore 0:
  10.0 132.9 all-gather.4
  144.9 68.7 all-gather.6
  264.5 35.8 all-gather.8
  302.7 36.7 all-gather.10
  360.5 51.3 reduce-scatter.9
  416.0 51.2 reduce-scatter.7
  477.0 71.2 reduce-scatter.13
  590.8 156.0 reduce-scatter.11
  750.2 34.1 reduce-scatter.15
  788.3 436.9 all-reduce.4
